TPU v7x, 32 devices: a whole 2x2x4 slice. The times are simulated.
32 devices in a mesh: ord: 8 (over y, x, core), ch: 4 (over z).
Axes of the slice: x: 2, y: 2, z: 4, core: 2. Of those that a mesh axis runs over, the one named last changes fastest.
Arguments:
- field_grid: bfloat16 [2, 64, 2, 352, 1440], P(None, 'ch', None, 'ord'), may hold values from -40 to 40
- norm_gain: float32 [64], P('ch'), may hold values from 0.1 to 1.9
- norm_bias: float32 [64], P('ch'), may hold values from -3 to 3
- order_table: int32 [512], replicated, may hold values from 0 to 511, as said below
- legendre: bfloat16 [512, 2, 352, 360], P(('ord', 'ch')), may hold values from -0.3125 to 0.3125
Outputs:
- coefficients: bfloat16 [512, 2, 2, 2, 64, 360], P(('ord', 'ch'))
Inputs may be any that keep to these rules, and one draw needn't show every extreme that they name: `order_table`: a permutation of the orders in which slots 2 q and 2 q + 1 hold orders p and 511 - p.
All inputs are finite; a program needn't handle non-finite values.
Results may differ from a plain program's by a relative error of at most 0.0062.
Values may be sent and summed in bfloat16 or wider, within the bound.
A program may use at most 128 MiB of HBM per device.

v0:
```python
from functools import partial
import math
import jax
import jax.numpy as jnp
from jax import lax
from jax.sharding import PartitionSpec as P


def slot_table(orders, length):
    sample = jnp.arange(length, dtype=jnp.int32)
    phases = sample[:, None] * orders[None, :] % length
    angles = phases.astype(jnp.float32) * (2.0 * math.pi / length)
    factor = 1.0 / math.sqrt(length)
    stacked = jnp.stack([jnp.cos(angles) * factor, -jnp.sin(angles) * factor], axis=2)
    return stacked.reshape(length, 2 * orders.shape[0]).astype(jnp.bfloat16)


def legendre_sums(arrived, legendre, orders):
    odd_order = orders % 2 == 1
    swapped = jnp.where(
        odd_order[:, None, None, None, None, None], arrived[:, :, :, :, ::-1], arrived
    )
    raw_sums = jnp.einsum(
        "srbcpi,spij->sprbcj", swapped, legendre, preferred_element_type=jnp.float32
    )
    half_degrees = legendre.shape[3]
    degree = (
        2 * jnp.arange(half_degrees, dtype=jnp.int32)[None, :]
        + jnp.arange(2, dtype=jnp.int32)[:, None]
    )
    allowed = degree[None, :, :] >= orders[:, None, None]
    return jnp.where(allowed[:, :, None, None, None, :], raw_sums, 0.0).astype(jnp.bfloat16)


def on_device(field_grid, norm_gain, norm_bias, order_table, legendre):
    batch_size, chan_local, hemis, cycle_local, longitudes = field_grid.shape
    order_total = order_table.shape[0]
    values = field_grid.astype(jnp.float32)
    cell_count = hemis * cycle_local * lax.axis_size("ord") * longitudes
    partial_sum = jnp.sum(values, axis=(2, 3, 4))
    totals, squares = lax.psum((partial_sum, jnp.sum(values * values, axis=(2, 3, 4))), "ord")
    average = totals / cell_count
    spread = squares / cell_count - average * average
    centered = values - average[:, :, None, None, None]
    inverse_scale = lax.rsqrt(spread + 1e-05) * norm_gain[None, :]
    normed = (
        centered * inverse_scale[:, :, None, None, None] + norm_bias[None, :, None, None, None]
    ).astype(jnp.bfloat16)
    twiddle = slot_table(order_table, longitudes)
    flat_rows = normed.reshape(-1, longitudes)
    fourier = lax.dot_general(
        twiddle, flat_rows, (((0,), (1,)), ((), ())), preferred_element_type=jnp.float32
    )
    fourier = fourier.reshape(order_total, 2, batch_size, chan_local, hemis, cycle_local)
    north = fourier[:, :, :, :, 0]
    south = fourier[:, :, :, :, 1]
    halves = jnp.stack([north + south, north - south], axis=4).astype(jnp.bfloat16)
    slot_count = legendre.shape[0]
    channel_groups = lax.axis_size("ch")
    first_slot = (lax.axis_index("ord") * channel_groups + lax.axis_index("ch")) * slot_count
    own_orders = lax.dynamic_slice_in_dim(order_table, first_slot, slot_count)
    transform = partial(legendre_sums, legendre=legendre, orders=own_orders)
    arrived = lax.all_to_all(
        lax.all_to_all(halves, "ord", split_axis=0, concat_axis=5, tiled=True),
        "ch",
        split_axis=0,
        concat_axis=3,
        tiled=True,
    )
    return transform(arrived)


def solution(mesh):
    placed = (
        P(None, "ch", None, "ord", None),
        P("ch"),
        P("ch"),
        P(),
        P(("ord", "ch"), None, None, None),
    )
    return jax.shard_map(
        on_device,
        mesh=mesh,
        in_specs=placed,
        out_specs=P(("ord", "ch"), None, None, None, None, None),
        check_vma=False,
    )
```

profile of v0, /device:TPU:0, one launch (start us, length us, event | category | flops | bytes accessed | tf_op | source)
XLA Modules:
  0.0 532.1 jit_solution(7866468105255323386)
XLA Ops:
  0.0 0.0 copy-start
  0.0 21.6 %convert_reduce_fusion = (f32[2,16]{1,0:T(2,128)S(1)}, f32[2,16]{1,0:T(2,128)S(1)}) fusion(bf16[2,16,2,44,1440]{4,2,3,1,0:T(2,128)(2,1)} %param.5), kind=kLoop, calls=%fused_computation.2 | loop fusion | flops 16220096 | bytes 8110336 | tf_op jit(solution)/shard_map/reduce_sum | solution.py:40
  21.6 0.0 copy-done
  21.6 12.8 %multiply_convert_fusion.1 = (bf16[1440,512,1]{1,0,2:T(8,128)(2,1)S(1)}, bf16[1440,512,1]{1,0,2:T(8,128)(2,1)S(1)}) fusion(s32[512]{0:T(512)S(1)} %copy-done), kind=kLoop, calls=%fused_computation.24 | loop fusion | flops 10321920 | bytes 2951168 | tf_op jit(solution)/shard_map/convert.2
  34.3 1.9 pad_maximum_fusion.1
  36.2 7.4 %copy.27 = bf16[1440,512,2]{0,2,1:T(2,128)(2,1)S(1)} copy(bf16[1440,512,2]{1,0,2:T(8,128)(2,1)} %pad_maximum_fusion.1) | data formatting | bytes 5898240 | tf_op jit(solution)/shard_map/stack | solution.py:14
  43.6 0.0 copy-start.2
  43.6 0.0 copy-start.1
  43.6 3.5 convert_element_type.29
  47.2 6.1 %dot_general.11 = bf16[512,2,1440]{2,1,0:T(2,128)(2,1)S(1)} reshape(bf16[1024,1440]{1,0:T(8,128)(2,1)} %bitcast.26) | data formatting | bytes 5898240 | tf_op jit(solution)/shard_map/dot_general | solution.py:51
  53.3 15.3 %all-reduce = (f32[2,16]{1,0:T(2,128)S(1)}, f32[2,16]{1,0:T(2,128)S(1)}) all-reduce(f32[2,16]{1,0:T(2,128)S(1)} %get-tuple-element.6, f32[2,16]{1,0:T(2,128)S(1)} %get-tuple-element.5), channel_id=1, replica_groups=mesh['ord'=8,'ch'=4] {'ord'}, use_global_device_ids=true, to_apply=%region_3.0 | all-reduce | flops 64 | bytes 512 | tf_op jit(solution)/shard_map/psum | solution.py:41
  68.7 0.0 copy-done.2
  68.7 0.0 copy-done.1
  68.7 14.5 %fusion.2 = bf16[2,16,2,44,1440]{4,2,3,1,0:T(2,128)(2,1)} fusion(bf16[2,16,2,44,1440]{4,2,3,1,0:T(2,128)(2,1)} %param.5, f32[16]{0:T(128)S(1)} %copy-done.1, f32[2,16]{1,0:T(2,128)S(1)} %get-tuple-element.16, f32[2,16]{1,0:T(2,128)S(1)} %get-tuple-element.15), kind=kLoop, calls=%fused_computation.5 | loop fusion | flops 20275200 | bytes 16220480 | tf_op jit(solution)/shard_map/convert_element_type | solution.py:48
  83.2 12.6 %fusion.4 = f32[512,2,2,16,2,44]{0,5,4,3,2,1:T(8,128)S(1)} fusion(bf16[2,16,2,44,1440]{4,2,3,1,0:T(2,128)(2,1)} %fusion.2, bf16[512,2,1440,1,1,1]{2,1,0,5,4,3:T(2,128)(2,1)S(1)} %bitcast.27), kind=kOutput, calls=%fused_computation.9 | convolution fusion | flops 8304721920 | bytes 22593536 | tf_op jit(solution)/shard_map/dot_general | solution.py:51
  95.8 2.3 add_convert_fusion
  98.1 3.3 pad_maximum_fusion
  101.4 40.4 %copy.30 = bf16[512,2,2,16,2,44]{5,4,3,2,1,0:T(2,128)(2,1)} copy(bf16[512,2,2,16,2,44]{0,5,4,3,2,1:T(8,128)(2,1)} %pad_maximum_fusion) | data formatting | bytes 11534336 | tf_op jit(solution)/shard_map/stack | solution.py:57
  141.8 46.0 %reshape.129 = bf16[8,2,180224]{2,1,0:T(2,128)(2,1)} reshape(bf16[512,2,2,16,2,44]{5,4,3,2,1,0:T(2,128)(2,1)} %copy.30) | data formatting | bytes 11534336
  187.9 71.0 %all_to_all.36 = bf16[8,2,180224]{2,1,0:T(2,128)(2,1)} all-to-all(bf16[8,2,180224]{2,1,0:T(2,128)(2,1)} %reshape.129), channel_id=1, replica_groups=mesh['ord'=8,'ch'=4] {'ord'}, dimensions={0} | all-to-all | bytes 11534336 | tf_op jit(solution)/shard_map/all_to_all | solution.py:64
  258.8 50.2 %reshape.130 = bf16[512,2,2,16,2,44]{5,4,3,2,1,0:T(2,128)(2,1)} reshape(bf16[8,2,180224]{2,1,0:T(2,128)(2,1)} %all_to_all.36) | data formatting | bytes 11534336
  309.0 44.8 %copy.41 = bf16[8,64,2,2,16,2,44]{1,4,6,0,5,3,2:T(8,128)(2,1)} copy(bf16[8,64,2,2,16,2,44]{6,5,4,3,2,1,0:T(2,128)(2,1)} %bitcast.23) | data formatting | bytes 11534336 | tf_op jit(solution)/shard_map/all_to_all | solution.py:64
  353.8 18.0 %copy.33 = bf16[64,2,2,16,2,352]{5,3,4,2,1,0:T(8,128)(2,1)} copy(bf16[64,2,2,16,2,352]{0,3,5,4,2,1:T(8,128)(2,1)} %bitcast.24) | data formatting | bytes 11534336 | tf_op jit(solution)/shard_map/all_to_all | solution.py:64
  371.8 5.5 %all-to-all-start.1 = ((bf16[64,2,2,16,2,352]{5,3,4,2,1,0:T(8,128)(2,1)}), bf16[64,2,2,16,2,352]{5,3,4,2,1,0:T(8,128)(2,1)}, u32[]{:S(2)}, u32[]{:S(2)}) async-start(bf16[64,2,2,16,2,352]{5,3,4,2,1,0:T(8,128)(2,1)} %copy.33), calls=%async_computation.1 | async-start | bytes 12582912 | tf_op jit(solution)/shard_map/all_to_all | solution.py:63
  377.4 0.1 fusion.20
  377.5 0.1 broadcast_compare_fusion
  377.6 137.6 %all-to-all-done.1 = bf16[64,2,2,16,2,352]{5,3,4,2,1,0:T(8,128)(2,1)} async-done(((bf16[64,2,2,16,2,352]{5,3,4,2,1,0:T(8,128)(2,1)}), bf16[64,2,2,16,2,352]{5,3,4,2,1,0:T(8,128)(2,1)}, u32[]{:S(2)}, u32[]{:S(2)}) %all-to-all-start.1) | async-done | bytes 5767200 | tf_op jit(solution)/shard_map/all_to_all | solution.py:63
  515.2 4.0 copy.34
  519.1 3.3 reverse_select_fusion
  522.4 9.7 %select_convert_fusion = bf16[16,2,2,2,64,360]{5,4,3,2,1,0:T(8,128)(2,1)} fusion(pred[16,2,360]{2,1,0:T(4,128)(4,1)S(1)} %broadcast_compare_fusion, bf16[16,2,352,360]{3,2,1,0:T(8,128)(2,1)} %param.9, bf16[16,2,2,64,2,352]{5,3,4,2,1,0:T(8,128)(2,1)S(1)} %reverse_select_fusion), kind=kOutput, calls=%fused_computation.7 | convolution fusion | flops 2082078720 | bytes 19787008 | tf_op jit(solution)/shard_map/srbcpi,spij->sprbcj/dot_general | solution.py:23
  (3 shorter events, 0.0 us)
Async XLA Ops:
  0.0 21.6 %copy-start = (s32[512]{0:T(512)S(1)}, s32[512]{0:T(512)}, u32[]{:S(2)}) copy-start(s32[512]{0:T(512)} %param.8) | copy-start | bytes 6148
  43.6 25.0 %copy-start.2 = (f32[16]{0:T(128)S(1)}, f32[16]{0:T(128)}, u32[]{:S(2)}) copy-start(f32[16]{0:T(128)} %param.6) | copy-start | bytes 196
  43.6 25.0 %copy-start.1 = (f32[16]{0:T(128)S(1)}, f32[16]{0:T(128)}, u32[]{:S(2)}) copy-start(f32[16]{0:T(128)} %param.7) | copy-start | bytes 196
  371.8 143.3 %all-to-all-start.1 = ((bf16[64,2,2,16,2,352]{5,3,4,2,1,0:T(8,128)(2,1)}), bf16[64,2,2,16,2,352]{5,3,4,2,1,0:T(8,128)(2,1)}, u32[]{:S(2)}, u32[]{:S(2)}) async-start(bf16[64,2,2,16,2,352]{5,3,4,2,1,0:T(8,128)(2,1)} %copy.33), calls=%async_computation.1 | async-start | bytes 12582912 | tf_op jit(solution)/shard_map/all_to_all | solution.py:63
where the time goes:
time: 536 us; the launch traced here: 532 us
  local copies, waits for them, and re-layouts  220 us (41%)
  waiting for transfers between devices  138 us (26%)
  blocking collectives  86.3 us (16%)
  other arithmetic  59.8 us (11%)
  matrix products  22.3 us (4%)
  starting transfers between devices  5.52 us (1%)
    all_to_all x1, waiting for transfers between devices, on_device(): lax.all_to_all(lax.all_to_all(halves, 'ord', split_axis=0, concat_axis=5,...  138 us
    unnamed x8, local copies, waits for them, and re-layouts  96.2 us
    all_to_all x1, blocking collectives, on_device(): lax.all_to_all(halves, 'ord', split_axis=0, concat_axis=5, tiled=True)  71 us
    all_to_all x2, local copies, waits for them, and re-layouts, on_device(): lax.all_to_all(halves, 'ord', split_axis=0, concat_axis=5, tiled=True)  62.8 us
    another operation x1, local copies, waits for them, and re-layouts, on_device(): jnp.stack([north + south, north - south], axis=4).astype(jnp.bfloat16)  40.4 us
    reduce_sum x1, other arithmetic, on_device(): partial_sum = jnp.sum(values, axis=(2, 3, 4))  21.6 us
    psum x1, blocking collectives, on_device(): lax.psum((partial_sum, jnp.sum(values * values, axis=(2, 3, 4))), 'ord')  15.3 us
    another operation x2, other arithmetic  15 us
  transfers between devices with their start and end apart: 1, of which 1 were waited for; matrix products, arithmetic and copies ran while one was open for 0% of the time, Pallas kernels for 0%

commit v1 on v0

--- a/solution.py
+++ b/solution.py
@@ -4,6 +4,13 @@
 import jax.numpy as jnp
 from jax import lax
 from jax.sharding import PartitionSpec as P
+
+
+def trade_parts(value, mesh_axis, split, join):
+    size = lax.axis_size(mesh_axis)
+    blocks = jnp.stack(jnp.split(value, size, axis=split), axis=0)
+    blocks = lax.all_to_all(blocks, mesh_axis, split_axis=0, concat_axis=0)
+    return jnp.concatenate(blocks, axis=join)
 
 
 def slot_table(orders, length):
@@ -60,12 +67,8 @@
     first_slot = (lax.axis_index("ord") * channel_groups + lax.axis_index("ch")) * slot_count
     own_orders = lax.dynamic_slice_in_dim(order_table, first_slot, slot_count)
     transform = partial(legendre_sums, legendre=legendre, orders=own_orders)
-    arrived = lax.all_to_all(
-        lax.all_to_all(halves, "ord", split_axis=0, concat_axis=5, tiled=True),
-        "ch",
-        split_axis=0,
-        concat_axis=3,
-        tiled=True,
+    arrived = trade_parts(
+        lax.all_to_all(halves, "ord", split_axis=0, concat_axis=5, tiled=True), "ch", 0, 3
     )
     return transform(arrived)
 

time: 536 us -> 654 us (1.22)
  local copies, waits for them, and re-layouts: 220 us -> 327 us
    split x0 -> x5, local copies, waits for them, and re-layouts: none -> 102 us  [trade_parts(): blocks = jnp.stack(jnp.split(value, size, axis=split), axis=0)]
    another operation x0 -> x4, local copies, waits for them, and re-layouts: none -> 23.9 us  [trade_parts(): blocks = jnp.stack(jnp.split(value, size, axis=split), axis=0)]
    all_to_all x2 -> x1, local copies, waits for them, and re-layouts: 62.8 us -> 43.3 us  [on_device(): lax.all_to_all(halves, 'ord', split_axis=0, concat_axis=5, tiled=True)]
    another operation x2 -> x3, other arithmetic: 15 us -> 20.7 us
where the time goes in v1:
time: 654 us; the launch traced here: 645 us
  local copies, waits for them, and re-layouts  327 us (50%)
  waiting for transfers between devices  138 us (21%)
  blocking collectives  86.6 us (13%)
  other arithmetic  65.4 us (10%)
  matrix products  22.3 us (3%)
    all_to_all x1, waiting for transfers between devices, trade_parts(): blocks = lax.all_to_all(blocks, mesh_axis, split_axis=0, concat_axis=0)  138 us
    split x5, local copies, waits for them, and re-layouts, trade_parts(): blocks = jnp.stack(jnp.split(value, size, axis=split), axis=0)  102 us
    unnamed x8, local copies, waits for them, and re-layouts  96.7 us
    all_to_all x1, blocking collectives, on_device(): lax.all_to_all(halves, 'ord', split_axis=0, concat_axis=5, tiled=True)  71.2 us
    all_to_all x1, local copies, waits for them, and re-layouts, on_device(): lax.all_to_all(halves, 'ord', split_axis=0, concat_axis=5, tiled=True)  43.3 us
    another operation x1, local copies, waits for them, and re-layouts, on_device(): jnp.stack([north + south, north - south], axis=4).astype(jnp.bfloat16)  40.3 us
    another operation x4, local copies, waits for them, and re-layouts, trade_parts(): blocks = jnp.stack(jnp.split(value, size, axis=split), axis=0)  23.9 us
    reduce_sum x1, other arithmetic, on_device(): partial_sum = jnp.sum(values, axis=(2, 3, 4))  21.6 us
  transfers between devices with their start and end apart: 1, of which 1 were waited for; matrix products, arithmetic and copies ran while one was open for 0% of the time, Pallas kernels for 0%

profile of v1, /device:TPU:0, one launch (start us, length us, event | category | flops | bytes accessed | tf_op | source)
XLA Modules:
  0.0 644.7 jit_solution(17531438197373314975)
XLA Ops:
  0.0 0.0 copy-start
  0.0 21.6 %convert_reduce_fusion = (f32[2,16]{1,0:T(2,128)S(1)}, f32[2,16]{1,0:T(2,128)S(1)}) fusion(bf16[2,16,2,44,1440]{4,2,3,1,0:T(2,128)(2,1)} %param.5), kind=kLoop, calls=%fused_computation.2 | loop fusion | flops 16220096 | bytes 8110336 | tf_op jit(solution)/shard_map/reduce_sum | solution.py:47
  21.6 0.0 copy-done
  21.6 12.8 %multiply_convert_fusion.1 = (bf16[1440,512,1]{1,0,2:T(8,128)(2,1)S(1)}, bf16[1440,512,1]{1,0,2:T(8,128)(2,1)S(1)}) fusion(s32[512]{0:T(512)S(1)} %copy-done), kind=kLoop, calls=%fused_computation.25 | loop fusion | flops 10321920 | bytes 2951168 | tf_op jit(solution)/shard_map/convert.2
  34.3 1.9 pad_maximum_fusion.2
  36.2 7.4 %copy.33 = bf16[1440,512,2]{0,2,1:T(2,128)(2,1)S(1)} copy(bf16[1440,512,2]{1,0,2:T(8,128)(2,1)} %pad_maximum_fusion.2) | data formatting | bytes 5898240 | tf_op jit(solution)/shard_map/stack | solution.py:21
  43.6 0.0 copy-start.2
  43.6 0.0 copy-start.1
  43.6 3.5 convert_element_type.29
  47.2 6.1 dot_general.11
  53.3 15.4 %all-reduce = (f32[2,16]{1,0:T(2,128)S(1)}, f32[2,16]{1,0:T(2,128)S(1)}) all-reduce(f32[2,16]{1,0:T(2,128)S(1)} %get-tuple-element.6, f32[2,16]{1,0:T(2,128)S(1)} %get-tuple-element.5), channel_id=1, replica_groups=mesh['ord'=8,'ch'=4] {'ord'}, use_global_device_ids=true, to_apply=%region_3.0 | all-reduce | flops 64 | bytes 512 | tf_op jit(solution)/shard_map/psum | solution.py:48
  68.8 0.0 copy-done.2
  68.8 0.0 copy-done.1
  68.8 14.5 %fusion.2 = bf16[2,16,2,44,1440]{4,2,3,1,0:T(2,128)(2,1)} fusion(bf16[2,16,2,44,1440]{4,2,3,1,0:T(2,128)(2,1)} %param.5, f32[16]{0:T(128)S(1)} %copy-done.1, f32[2,16]{1,0:T(2,128)S(1)} %get-tuple-element.20, f32[2,16]{1,0:T(2,128)S(1)} %get-tuple-element.19), kind=kLoop, calls=%fused_computation.5 | loop fusion | flops 20275200 | bytes 16220480 | tf_op jit(solution)/shard_map/convert_element_type | solution.py:55
  83.3 12.6 %fusion.4 = f32[512,2,2,16,2,44]{0,5,4,3,2,1:T(8,128)S(1)} fusion(bf16[2,16,2,44,1440]{4,2,3,1,0:T(2,128)(2,1)} %fusion.2, bf16[512,2,1440,1,1,1]{2,1,0,5,4,3:T(2,128)(2,1)S(1)} %bitcast.38), kind=kOutput, calls=%fused_computation.9 | convolution fusion | flops 8304721920 | bytes 22593536 | tf_op jit(solution)/shard_map/dot_general | solution.py:58
  95.9 2.3 add_convert_fusion
  98.2 3.3 pad_maximum_fusion
  101.5 40.3 %copy.36 = bf16[512,2,2,16,2,44]{5,4,3,2,1,0:T(2,128)(2,1)} copy(bf16[512,2,2,16,2,44]{0,5,4,3,2,1:T(8,128)(2,1)} %pad_maximum_fusion) | data formatting | bytes 11534336 | tf_op jit(solution)/shard_map/stack | solution.py:64
  141.9 46.5 %reshape.145 = bf16[8,2,180224]{2,1,0:T(2,128)(2,1)} reshape(bf16[512,2,2,16,2,44]{5,4,3,2,1,0:T(2,128)(2,1)} %copy.36) | data formatting | bytes 11534336
  188.4 71.2 %all_to_all.20 = bf16[8,2,180224]{2,1,0:T(2,128)(2,1)} all-to-all(bf16[8,2,180224]{2,1,0:T(2,128)(2,1)} %reshape.145), channel_id=1, replica_groups=mesh['ord'=8,'ch'=4] {'ord'}, dimensions={0} | all-to-all | bytes 11534336 | tf_op jit(solution)/shard_map/all_to_all | solution.py:71
  259.5 50.2 %reshape.146 = bf16[512,2,2,16,2,44]{5,4,3,2,1,0:T(2,128)(2,1)} reshape(bf16[8,2,180224]{2,1,0:T(2,128)(2,1)} %all_to_all.20) | data formatting | bytes 11534336
  309.7 43.3 %copy.48 = bf16[8,64,2,2,16,2,44]{1,0,4,6,5,3,2:T(8,128)(2,1)} copy(bf16[8,64,2,2,16,2,44]{6,5,4,3,2,1,0:T(2,128)(2,1)} %bitcast.35) | data formatting | bytes 11534336 | tf_op jit(solution)/shard_map/all_to_all | solution.py:71
  353.0 32.4 %fusion.22 = (bf16[16,2,2,16,2,8,44]{0,5,3,6,4,2,1:T(8,128)(2,1)}, bf16[16,2,2,16,2,8,44]{0,5,3,6,4,2,1:T(8,128)(2,1)}, bf16[16,2,2,16,2,8,44]{0,5,3,6,4,2,1:T(8,128)(2,1)}, bf16[16,2,2,16,2,8,44]{0,5,3,6,4,2,1:T(8,128)(2,1)}) fusion(bf16[64,2,2,16,2,8,44]{0,5,3,6,4,2,1:T(8,128)(2,1)} %bitcast.34), kind=kLoop, calls=%fused_computation.40 | loop fusion | bytes 11534336 | tf_op jit(solution)/shard_map/split | solution.py:11
  385.4 17.3 %copy.38 = bf16[16,2,2,16,2,8,44]{6,5,3,4,2,1,0:T(8,128)(2,1)} copy(bf16[16,2,2,16,2,8,44]{0,5,3,6,4,2,1:T(8,128)(2,1)} %get-tuple-element.13) | data formatting | bytes 2883584 | tf_op jit(solution)/shard_map/split | solution.py:11
  402.7 5.5 stack.29
  408.3 17.3 %copy.39 = bf16[16,2,2,16,2,8,44]{6,5,3,4,2,1,0:T(8,128)(2,1)} copy(bf16[16,2,2,16,2,8,44]{0,5,3,6,4,2,1:T(8,128)(2,1)} %get-tuple-element.16) | data formatting | bytes 2883584 | tf_op jit(solution)/shard_map/split | solution.py:11
  425.6 5.5 stack.30
  431.1 17.3 %copy.40 = bf16[16,2,2,16,2,8,44]{6,5,3,4,2,1,0:T(8,128)(2,1)} copy(bf16[16,2,2,16,2,8,44]{0,5,3,6,4,2,1:T(8,128)(2,1)} %get-tuple-element.15) | data formatting | bytes 2883584 | tf_op jit(solution)/shard_map/split | solution.py:11
  448.4 6.4 stack.31
  454.8 17.5 %copy.41 = bf16[16,2,2,16,2,8,44]{6,5,3,4,2,1,0:T(8,128)(2,1)} copy(bf16[16,2,2,16,2,8,44]{0,5,3,6,4,2,1:T(8,128)(2,1)} %get-tuple-element.14) | data formatting | bytes 2883584 | tf_op jit(solution)/shard_map/split | solution.py:11
  472.3 6.4 stack.32
  478.7 5.6 pad_maximum_fusion.1
  484.4 5.3 all-to-all-start.1
  489.6 0.1 fusion.20
  489.7 0.1 broadcast_compare_fusion
  489.8 137.6 %all-to-all-done.1 = bf16[4,16,2,2,16,2,352]{6,4,5,3,2,1,0:T(8,128)(2,1)} async-done(((bf16[4,16,2,2,16,2,352]{6,4,5,3,2,1,0:T(8,128)(2,1)}), bf16[4,16,2,2,16,2,352]{6,4,5,3,2,1,0:T(8,128)(2,1)}, u32[]{:S(2)}, u32[]{:S(2)}) %all-to-all-start.1) | async-done | bytes 5767200 | tf_op jit(solution)/shard_map/all_to_all | solution.py:12
  627.5 4.0 copy.42
  631.4 3.3 reverse_select_fusion
  634.7 9.7 %select_convert_fusion = bf16[16,2,2,2,64,360]{5,4,3,2,1,0:T(8,128)(2,1)} fusion(pred[16,2,360]{2,1,0:T(4,128)(4,1)S(1)} %broadcast_compare_fusion, bf16[16,2,352,360]{3,2,1,0:T(8,128)(2,1)} %param.9, bf16[16,2,2,64,2,352]{5,3,4,2,1,0:T(8,128)(2,1)S(1)} %reverse_select_fusion), kind=kOutput, calls=%fused_computation.7 | convolution fusion | flops 2082078720 | bytes 19787008 | tf_op jit(solution)/shard_map/srbcpi,spij->sprbcj/dot_general | solution.py:30
  (3 shorter events, 0.0 us)
Async XLA Ops:
  0.0 21.6 %copy-start = (s32[512]{0:T(512)S(1)}, s32[512]{0:T(512)}, u32[]{:S(2)}) copy-start(s32[512]{0:T(512)} %param.8) | copy-start | bytes 6148
  43.6 25.1 %copy-start.2 = (f32[16]{0:T(128)S(1)}, f32[16]{0:T(128)}, u32[]{:S(2)}) copy-start(f32[16]{0:T(128)} %param.6) | copy-start | bytes 196
  43.6 25.1 %copy-start.1 = (f32[16]{0:T(128)S(1)}, f32[16]{0:T(128)}, u32[]{:S(2)}) copy-start(f32[16]{0:T(128)} %param.7) | copy-start | bytes 196
  484.4 143.1 %all-to-all-start.1 = ((bf16[4,16,2,2,16,2,352]{6,4,5,3,2,1,0:T(8,128)(2,1)}), bf16[4,16,2,2,16,2,352]{6,4,5,3,2,1,0:T(8,128)(2,1)}, u32[]{:S(2)}, u32[]{:S(2)}) async-start(bf16[4,16,2,2,16,2,352]{6,4,5,3,2,1,0:T(8,128)(2,1)} %pad_maximum_fusion.1), calls=%async_computation.1 | async-start | bytes 12582912 | tf_op jit(solution)/shard_map/all_to_all | solution.py:12
